TPU v7x, 256 devices: a whole 4x4x8 slice. The times are simulated.
256 devices in a mesh: ctx: 32 (over x, y, core), head: 8 (over z).
Axes of the slice: x: 4, y: 4, z: 8, core: 2. Of those that a mesh axis runs over, the one named last changes fastest.
Arguments:
- queries: bfloat16 [2, 6144, 4096], P(None, 'ctx', 'head'), may hold values from -6 to 6
- key_rows: bfloat16 [2, 6144, 4096], P(None, 'ctx', 'head'), may hold values from -6 to 6
- value_rows: bfloat16 [2, 6144, 4096], P(None, 'ctx', 'head'), may hold values from -6 to 6
- out_weight: bfloat16 [4096, 4096], P('head'), may hold values from -0.09375 to 0.09375
- cotangent: bfloat16 [2, 6144, 4096], P(None, 'ctx', 'head'), may hold values from -6 to 6
Outputs:
- layer_output: bfloat16 [2, 6144, 4096], P(None, 'ctx', 'head')
- query_grad: bfloat16 [2, 6144, 4096], P(None, 'ctx', 'head')
- key_grad: bfloat16 [2, 6144, 4096], P(None, 'ctx', 'head')
- value_grad: bfloat16 [2, 6144, 4096], P(None, 'ctx', 'head')
- weight_grad: float32 [4096, 4096], P('head', 'ctx')
All inputs are finite; a program needn't handle non-finite values.
Results may differ from a plain program's by a relative error of at most 0.015.
Values may be sent and summed in bfloat16 or wider, within the bound.
No kernel may reach another device: no remote copies, remote signals or barrier semaphores. Data moves between devices by JAX's collectives and lax.ppermute only.
A program may use at most 128 MiB of HBM per device.

v0:
```python
import jax
import jax.numpy as jnp
from jax import lax
from jax.sharding import Mesh
from jax.sharding import PartitionSpec as P

DH = 128
CTX = ("ctx_0", "ctx_1", "ctx_2")
epsilon = 1e-06


def filled_with(value, identity):
    return jnp.broadcast_to(jnp.asarray(identity, value.dtype), value.shape)


def prefix_by_axis(value, axes, combine, identity, reverse):
    before = start = filled_with(value, identity)
    subtotal = value
    for axis in reversed(axes):
        count, index = (lax.axis_size(axis), lax.axis_index(axis))
        pieces = lax.all_gather(subtotal, axis)
        inside, subtotal = (start, start)
        for k in reversed(range(count)) if reverse else range(count):
            passed = k > index if reverse else k < index
            subtotal = combine(subtotal, pieces[k])
            inside = jnp.where(passed, subtotal, inside)
        before = combine(inside, before)
    return before


def in_blocks(value, dim, count):
    before, after = (value.shape[:dim], value.shape[dim + 1 :])
    return jnp.moveaxis(value.reshape(*before, count, -1, *after), dim, 0)


def sum_at_owner(value, axis, dim):
    pieces = in_blocks(value, dim, lax.axis_size(axis))
    arrived = lax.all_to_all(pieces, axis, split_axis=0, concat_axis=0, tiled=True)
    return arrived.astype(jnp.float32).sum(axis=0)


def split_heads(array):
    length = array.shape[1]
    return array.reshape(2, length, array.shape[2] // DH, DH).transpose(0, 2, 1, 3)


def join_heads(array):
    length = array.shape[2]
    return array.transpose(0, 2, 1, 3).reshape(2, length, array.shape[1] * DH)


def rms_normalize(attended):
    return attended / jnp.sqrt(jnp.mean(attended * attended, axis=-1, keepdims=True) + epsilon)


def add_states(earlier, later):
    return earlier + later


def shards(queries, key_rows, value_rows, out_weight, cotangent):
    head_scale = DH ** (-0.5)
    length = queries.shape[1]
    rows_index = lax.broadcasted_iota(jnp.int32, (length, length), 0)
    cols_index = lax.broadcasted_iota(jnp.int32, (length, length), 1)
    lower = rows_index >= cols_index
    query_heads = split_heads(queries)
    key_heads = split_heads(key_rows)
    value_heads = split_heads(value_rows)
    raw = (
        jnp.einsum("bhtd,bhsd->bhts", query_heads, key_heads, preferred_element_type=jnp.float32)
        * head_scale
    )
    scores = jnp.where(lower, raw, 0.0).astype(jnp.bfloat16)
    local_state = jnp.einsum(
        "bhsd,bhse->bhde", key_heads, value_heads, preferred_element_type=jnp.float32
    )
    state = prefix_by_axis(local_state, CTX, add_states, jnp.zeros_like(local_state), False)
    state_bf = state.astype(jnp.bfloat16)
    attended = jnp.einsum(
        "bhts,bhsd->bhtd", scores, value_heads, preferred_element_type=jnp.float32
    )
    attended = attended + head_scale * jnp.einsum(
        "bhtd,bhde->bhte", query_heads, state_bf, preferred_element_type=jnp.float32
    )
    normed_flat = join_heads(rms_normalize(attended).astype(jnp.bfloat16))
    partial_value = jnp.einsum(
        "btr,rc->btc", normed_flat, out_weight, preferred_element_type=jnp.float32
    )
    layer_output = sum_at_owner(partial_value.astype(jnp.bfloat16), "head", 2).astype(jnp.bfloat16)
    grad_all = lax.all_gather(cotangent, "head", axis=2, tiled=True)
    normed_grad = jnp.einsum(
        "btc,rc->btr", grad_all, out_weight, preferred_element_type=jnp.float32
    )
    weight_term = jnp.einsum(
        "btr,btc->rc", normed_flat, grad_all, preferred_element_type=jnp.float32
    )
    token_factor = (2 * length * lax.axis_size(CTX)) ** (-0.5)
    weight_grad = (
        lax.psum_scatter(
            weight_term.astype(jnp.bfloat16), CTX, scatter_dimension=1, tiled=True
        ).astype(jnp.float32)
        * token_factor
    )
    pullback = jax.vjp(rms_normalize, attended)[1]
    attended_grad = pullback(split_heads(normed_grad))[0].astype(jnp.bfloat16)
    local_grad_state = jnp.einsum(
        "bhtd,bhte->bhde", query_heads, attended_grad, preferred_element_type=jnp.float32
    )
    grad_state = prefix_by_axis(
        local_grad_state, CTX, add_states, jnp.zeros_like(local_grad_state), True
    )
    grad_state_bf = grad_state.astype(jnp.bfloat16)
    raw_grad = (
        jnp.einsum(
            "bhtd,bhsd->bhts", attended_grad, value_heads, preferred_element_type=jnp.float32
        )
        * head_scale
    )
    score_grad = jnp.where(lower, raw_grad, 0.0).astype(jnp.bfloat16)
    query_part = jnp.einsum(
        "bhts,bhsd->bhtd", score_grad, key_heads, preferred_element_type=jnp.float32
    )
    query_part = query_part + head_scale * jnp.einsum(
        "bhte,bhde->bhtd", attended_grad, state_bf, preferred_element_type=jnp.float32
    )
    key_part = jnp.einsum(
        "bhts,bhtd->bhsd", score_grad, query_heads, preferred_element_type=jnp.float32
    )
    key_part = key_part + head_scale * jnp.einsum(
        "bhse,bhde->bhsd", value_heads, grad_state_bf, preferred_element_type=jnp.float32
    )
    value_part = jnp.einsum(
        "bhts,bhte->bhse", scores, attended_grad, preferred_element_type=jnp.float32
    )
    value_part = value_part + head_scale * jnp.einsum(
        "bhsd,bhde->bhse", key_heads, grad_state_bf, preferred_element_type=jnp.float32
    )
    query_grad = join_heads(query_part.astype(jnp.bfloat16))
    key_grad = join_heads(key_part.astype(jnp.bfloat16))
    value_grad = join_heads(value_part.astype(jnp.bfloat16))
    return (layer_output, query_grad, key_grad, value_grad, weight_grad)


def solution(mesh):
    split = Mesh(
        mesh.devices.reshape(4, 4, 2, mesh.shape["head"]), ("ctx_0", "ctx_1", "ctx_2", "head")
    )
    placed = (
        P(None, CTX, "head"),
        P(None, CTX, "head"),
        P(None, CTX, "head"),
        P("head", None),
        P(None, CTX, "head"),
    )
    return jax.shard_map(
        shards,
        mesh=split,
        in_specs=placed,
        out_specs=(
            P(None, CTX, "head"),
            P(None, CTX, "head"),
            P(None, CTX, "head"),
            P(None, CTX, "head"),
            P("head", CTX),
        ),
        check_vma=False,
    )
```

profile of v0, /device:TPU:1, one launch (start us, length us, event | category | flops | bytes accessed | tf_op | source)
XLA Modules:
  0.0 345.1 jit_solution(2595999831184184508)
XLA Ops:
  8.2 2.1 fusion.34
  10.4 19.0 %all-gather.18.cloned.1.call-done = f32[4,4,128,128]{3,2,1,0:T(8,128)} async-done(((f32[2,4,128,128]{3,2,1,0:T(8,128)}), f32[4,4,128,128]{3,2,1,0:T(8,128)}) %all-gather.18.cloned.1.call-update) | async-done | bytes 1048592 | tf_op jit(solution)/shard_map/all_gather | solution.py:21
  29.4 2.1 slice_add_fusion.13
  32.2 33.1 %all-gather.22.cloned.1.call-done = f32[8,4,128,128]{3,2,1,0:T(8,128)} async-done(((f32[2,4,128,128]{3,2,1,0:T(8,128)}), f32[8,4,128,128]{3,2,1,0:T(8,128)}) %all-gather.22.cloned.1.call-update) | async-done | bytes 2097168 | tf_op jit(solution)/shard_map/all_gather | solution.py:21
  65.4 2.4 fusion.31
  69.8 42.0 %all-gather.14.cloned.1.call-done = bf16[2,192,4096]{2,1,0:T(8,128)(2,1)} async-done(((bf16[2,192,512]{2,1,0:T(8,128)(2,1)}), bf16[2,192,4096]{2,1,0:T(8,128)(2,1)}) %all-gather.14.cloned.1.call-update) | async-done | bytes 3145744 | tf_op jit(solution)/shard_map/all_gather | solution.py:90
  111.8 5.9 %fusion.3 = f32[2,24,4,8,128]{4,3,2,1,0:T(8,128)} fusion(bf16[2,192,4096]{2,1,0:T(8,128)(2,1)} %all-gather.14.cloned.1.call-done, bf16[512,4096]{1,0:T(8,128)(2,1)} %param.8), kind=kOutput, calls=%fused_computation.8 | convolution fusion | flops 1610612736 | bytes 8126464 | tf_op jit(solution)/shard_map/btc,rc->btr/dot_general | solution.py:91
  117.7 28.1 %all-gather.12.cloned.1.call-done = f32[4,2,4,128,128]{4,3,2,1,0:T(8,128)} async-done(((f32[1,2,4,128,128]{4,3,2,1,0:T(8,128)}), f32[4,2,4,128,128]{4,3,2,1,0:T(8,128)}) %all-gather.12.cloned.1.call-update) | async-done | bytes 2097168 | tf_op jit(solution)/shard_map/all_gather | solution.py:21
  145.8 2.2 fusion.30
  152.6 15.4 %all-gather.20.cloned.1.call-done = f32[4,4,128,128]{3,2,1,0:T(8,128)} async-done(((f32[2,4,128,128]{3,2,1,0:T(8,128)}), f32[4,4,128,128]{3,2,1,0:T(8,128)}) %all-gather.20.cloned.1.call-update) | async-done | bytes 1048592 | tf_op jit(solution)/shard_map/all_gather | solution.py:21
  168.0 2.1 slice_add_fusion.6
  170.4 6.3 %bitcast_convert_fusion = bf16[512,4096]{1,0:T(8,128)(2,1)} fusion(bf16[2,192,4096]{2,1,0:T(8,128)(2,1)} %all-gather.14.cloned.1.call-done, bf16[2,4,24,8,128]{4,3,2,1,0:T(8,128)(2,1)S(1)} %fusion.37), kind=kOutput, calls=%fused_computation | convolution fusion | flops 1612709888 | bytes 7733248 | tf_op jit(solution)/shard_map/btr,btc->rc/dot_general | solution.py:94
  176.7 6.5 %copy.41 = bf16[512,4096]{0,1:T(8,128)(2,1)} copy(bf16[512,4096]{1,0:T(8,128)(2,1)} %bitcast_convert_fusion) | data formatting | bytes 8388608
  183.2 4.2 %convolution_convert_fusion = bf16[2,192,4096]{2,1,0:T(8,128)(2,1)S(1)} fusion(bf16[512,4096]{1,0:T(8,128)(2,1)} %param.8, bf16[2,4,24,8,128]{4,3,2,1,0:T(8,128)(2,1)S(1)} %fusion.37), kind=kOutput, calls=%fused_computation.1 | convolution fusion | flops 1612185600 | bytes 7733248 | tf_op jit(solution)/shard_map/btr,rc->btc/dot_general | solution.py:86
  187.4 2.0 copy.116
  189.4 6.5 %all-to-all-start = ((bf16[8,2,192,512]{3,2,1,0:T(8,128)(2,1)}), bf16[8,2,192,512]{3,2,1,0:T(8,128)(2,1)S(1)}, u32[]{:S(2)}, u32[]{:S(2)}) async-start(bf16[8,2,192,512]{3,2,1,0:T(8,128)(2,1)} %bitcast.230), calls=%async_computation | async-start | bytes 6291456 | tf_op jit(solution)/shard_map/all_to_all | solution.py:38
  196.1 7.8 %all-gather.24.cloned.1.call-done = f32[8,4,128,128]{3,2,1,0:T(8,128)} async-done(((f32[2,4,128,128]{3,2,1,0:T(8,128)}), f32[8,4,128,128]{3,2,1,0:T(8,128)}) %all-gather.24.cloned.1.call-update) | async-done | bytes 2097168 | tf_op jit(solution)/shard_map/all_gather | solution.py:21
  204.0 2.4 fusion.27
  206.5 1.5 select_convert_fusion
  208.0 1.6 fusion.36
  210.7 59.5 %all-to-all-done = bf16[8,2,192,512]{3,2,1,0:T(8,128)(2,1)S(1)} async-done(((bf16[8,2,192,512]{3,2,1,0:T(8,128)(2,1)}), bf16[8,2,192,512]{3,2,1,0:T(8,128)(2,1)S(1)}, u32[]{:S(2)}, u32[]{:S(2)}) %all-to-all-start) | async-done | bytes 3145760 | tf_op jit(solution)/shard_map/all_to_all | solution.py:38
  271.5 24.9 %reduce-scatter.4.cloned.1.call-done = bf16[128,512]{1,0:T(8,128)(2,1)} async-done(((bf16[4096,512]{1,0:T(8,128)(2,1)}), bf16[128,512]{1,0:T(8,128)(2,1)}) %reduce-scatter.4.cloned.1.call-update) | async-done | bytes 131088
  298.2 34.4 %all-gather.16.cloned.1.call-done = f32[4,2,4,128,128]{4,3,2,1,0:T(8,128)} async-done(((f32[1,2,4,128,128]{4,3,2,1,0:T(8,128)}), f32[4,2,4,128,128]{4,3,2,1,0:T(8,128)}) %all-gather.16.cloned.1.call-update) | async-done | bytes 2097168 | tf_op jit(solution)/shard_map/all_gather | solution.py:21
  332.5 3.0 fusion.26
  (75 shorter events, 15.8 us)
Async XLA Ops:
  7.2 22.2 %all-gather.18.cloned.1.call-start = ((), (), s32[]{:S(2)}) async-start(), calls=%async_computation.5 | async-start | bytes 1572864 | tf_op jit(solution)/shard_map/all_gather | solution.py:21
  10.3 58.2 %copy-start.6 = (bf16[2,192,512]{2,1,0:T(8,128)(2,1)S(1)}, bf16[2,192,512]{2,1,0:T(8,128)(2,1)}, u32[]{:S(2)}) copy-start(bf16[2,192,512]{2,1,0:T(8,128)(2,1)} %param.5) | copy-start | bytes 1179652
  10.3 58.2 %copy-start.9 = (bf16[2,192,512]{2,1,0:T(8,128)(2,1)S(1)}, bf16[2,192,512]{2,1,0:T(8,128)(2,1)}, u32[]{:S(2)}) copy-start(bf16[2,192,512]{2,1,0:T(8,128)(2,1)} %param.6) | copy-start | bytes 1179652
  10.3 55.0 %all-gather.22.cloned.1.call-start = ((), (), s32[]{:S(2)}) async-start(), calls=%async_computation.7 | async-start | bytes 2621440 | tf_op jit(solution)/shard_map/all_gather | solution.py:21
  31.4 80.4 %all-gather.14.cloned.1.call-start = ((), (), s32[]{:S(2)}) async-start(), calls=%async_computation.3 | async-start | bytes 3538944 | tf_op jit(solution)/shard_map/all_gather | solution.py:90
  32.2 113.6 %all-gather.12.cloned.1.call-start = ((), (), s32[]{:S(2)}) async-start(), calls=%async_computation.2 | async-start | bytes 2621440 | tf_op jit(solution)/shard_map/all_gather | solution.py:21
  67.8 100.2 %all-gather.20.cloned.1.call-start = ((), (), s32[]{:S(2)}) async-start(), calls=%async_computation.6 | async-start | bytes 1572864 | tf_op jit(solution)/shard_map/all_gather | solution.py:21
  69.8 76.0 %copy-start.1 = (f32[8,4,128,128]{3,2,1,0:T(8,128)S(1)}, f32[8,4,128,128]{3,2,1,0:T(8,128)}, u32[]{:S(2)}) copy-start(f32[8,4,128,128]{3,2,1,0:T(8,128)} %all-gather.22.cloned.1.call-done) | copy-start | bytes 6291460
  69.8 76.0 %copy-start.5 = (f32[4,4,128,128]{3,2,1,0:T(8,128)S(1)}, f32[4,4,128,128]{3,2,1,0:T(8,128)}, u32[]{:S(2)}) copy-start(f32[4,4,128,128]{3,2,1,0:T(8,128)} %all-gather.18.cloned.1.call-done) | copy-start | bytes 3145732
  145.8 2.2 copy-start.7
  145.8 2.5 copy-start.11
  148.0 1.9 copy-start.16
  148.0 1.2 copy-start.15
  152.5 51.5 %all-gather.24.cloned.1.call-start = ((), (), s32[]{:S(2)}) async-start(), calls=%async_computation.8 | async-start | bytes 2621440 | tf_op jit(solution)/shard_map/all_gather | solution.py:21
  170.1 126.3 %reduce-scatter.4.cloned.1.call-start = ((), (), s32[]{:S(2)}) async-start(), calls=%async_computation.9 | async-start | bytes 4325376
  189.4 80.8 %all-to-all-start = ((bf16[8,2,192,512]{3,2,1,0:T(8,128)(2,1)}), bf16[8,2,192,512]{3,2,1,0:T(8,128)(2,1)S(1)}, u32[]{:S(2)}, u32[]{:S(2)}) async-start(bf16[8,2,192,512]{3,2,1,0:T(8,128)(2,1)} %bitcast.230), calls=%async_computation | async-start | bytes 6291456 | tf_op jit(solution)/shard_map/all_to_all | solution.py:38
  195.9 136.6 %all-gather.16.cloned.1.call-start = ((), (), s32[]{:S(2)}) async-start(), calls=%async_computation.4 | async-start | bytes 2621440 | tf_op jit(solution)/shard_map/all_gather | solution.py:21
  206.5 3.1 copy-start.3
  206.5 3.1 copy-start.17
  207.9 2.0 copy-start.13
  271.5 64.1 %copy-start.10 = (bf16[2,192,512]{2,1,0:T(8,128)(2,1)S(1)}, bf16[2,192,512]{2,1,0:T(8,128)(2,1)}, u32[]{:S(2)}) copy-start(bf16[2,192,512]{2,1,0:T(8,128)(2,1)} %param.6) | copy-start | bytes 1179652
  298.2 38.0 %copy-start.4 = (bf16[2,4,192,128]{3,2,1,0:T(8,128)(2,1)S(1)}, bf16[2,4,192,128]{3,2,1,0:T(8,128)(2,1)}, u32[]{:S(2)}) copy-start(bf16[2,4,192,128]{3,2,1,0:T(8,128)(2,1)} %copy-done.2) | copy-start | bytes 1179652
  298.2 38.0 %copy-start.12 = (bf16[2,4,192,192]{3,2,1,0:T(8,128)(2,1)S(1)}, bf16[2,4,192,192]{3,2,1,0:T(8,128)(2,1)}, u32[]{:S(2)}) copy-start(bf16[2,4,192,192]{3,2,1,0:T(8,128)(2,1)} %select_convert_fusion.1) | copy-start | bytes 1769476
  335.6 1.2 copy-start.14
  (4 other events, 3.5 us)
Sparse Core Ops, SparseCore 0:
  10.5 18.8 all-gather.17
  31.6 33.7 all-gather.21
  67.2 44.6 all-gather.13
  113.5 32.3 all-gather.11
  152.7 15.3 all-gather.19
  170.2 33.7 all-gather.23
  207.9 88.4 reduce-scatter.3
  298.2 34.2 all-gather.15
where the time goes:
time: 346 us; the launch traced here: 345 us
  waiting for transfers between devices  265 us (77%)
  matrix products  25.8 us (7%)
  other arithmetic  17.6 us (5%)
  local copies, waits for them, and re-layouts  15.2 us (4%)
  between operations  14.5 us (4%)
  starting transfers between devices  7.02 us (2%)
    all_gather x6, waiting for transfers between devices, prefix_by_axis(): pieces = lax.all_gather(subtotal, axis)  138 us
    all_to_all x1, waiting for transfers between devices, sum_at_owner(): lax.all_to_all(pieces, axis, split_axis=0, concat_axis=0, tiled=True)  59.5 us
    all_gather x1, waiting for transfers between devices, shards(): grad_all = lax.all_gather(cotangent, 'head', axis=2, tiled=True)  42 us
    unnamed x9, waiting for transfers between devices  25.7 us
    unnamed x40, local copies, waits for them, and re-layouts  10.4 us
    add x4, other arithmetic, add_states(): return earlier + later  8.94 us
  transfers between devices with their start and end apart: 9, of which 9 were waited for; matrix products, arithmetic and copies ran while one was open for 11% of the time, Pallas kernels for 0%

commit v1 on v0

--- a/solution.py
+++ b/solution.py
@@ -7,6 +7,19 @@
 DH = 128
 CTX = ("ctx_0", "ctx_1", "ctx_2")
 epsilon = 1e-06
+
+
+def gather_around(array, axis, dim):
+    ways = lax.axis_size(axis)
+    up = [(d, (d + 1) % ways) for d in range(ways)]
+    down = [(d, (d - 1) % ways) for d in range(ways)]
+    earlier, later = ([array], [array])
+    for _ in range(ways // 2):
+        earlier.append(lax.ppermute(earlier[-1], axis, up))
+    for _ in range((ways - 1) // 2):
+        later.append(lax.ppermute(later[-1], axis, down))
+    line = jnp.concatenate([*earlier[::-1], *later[1:]], axis=dim)
+    return jnp.roll(line, (lax.axis_index(axis) - ways // 2) * array.shape[dim], axis=dim)
 
 
 def filled_with(value, identity):
@@ -87,7 +100,7 @@
         "btr,rc->btc", normed_flat, out_weight, preferred_element_type=jnp.float32
     )
     layer_output = sum_at_owner(partial_value.astype(jnp.bfloat16), "head", 2).astype(jnp.bfloat16)
-    grad_all = lax.all_gather(cotangent, "head", axis=2, tiled=True)
+    grad_all = gather_around(cotangent, "head", 2)
     normed_grad = jnp.einsum(
         "btc,rc->btr", grad_all, out_weight, preferred_element_type=jnp.float32
     )

time: 346 us -> 302 us (0.87)
  waiting for transfers between devices: 265 us -> 207 us
  starting transfers between devices: 7.02 us -> 17.2 us
  local copies, waits for them, and re-layouts: 15.2 us -> 19.8 us
    all_gather x6, waiting for transfers between devices: 138 us -> 92.4 us  [prefix_by_axis(): pieces = lax.all_gather(subtotal, axis)]
    all_gather x1 -> x0, waiting for transfers between devices: 42 us -> none  [shards(): grad_all = lax.all_gather(cotangent, 'head', axis=2, tiled=True)]
    ppermute x0 -> x7, waiting for transfers between devices: none -> 31.1 us  [the longest x4 19.4 us: gather_around(): earlier.append(lax.ppermute(earlier[-1], axis, up))]
    ppermute x0 -> x7, starting transfers between devices: none -> 10.3 us  [the longest x3 9.19 us: gather_around(): later.append(lax.ppermute(later[-1], axis, down))]
    unnamed x40 -> x57, local copies, waits for them, and re-layouts: 10.4 us -> 15 us
    unnamed x9 -> x8, waiting for transfers between devices: 25.7 us -> 24.7 us
  transfers between devices with their start and end apart: 9 -> 15, of which waited for: 9 -> 12; matrix products, arithmetic and copies ran while one was open for 11% -> 13% of each run, Pallas kernels for 0% -> 0%
where the time goes in v1:
time: 302 us; the launch traced here: 301 us
  waiting for transfers between devices  207 us (69%)
  matrix products  24.8 us (8%)
  local copies, waits for them, and re-layouts  19.8 us (7%)
  other arithmetic  17.7 us (6%)
  starting transfers between devices  17.2 us (6%)
  between operations  14.6 us (5%)
    all_gather x6, waiting for transfers between devices, prefix_by_axis(): pieces = lax.all_gather(subtotal, axis)  92.4 us
    all_to_all x1, waiting for transfers between devices, sum_at_owner(): lax.all_to_all(pieces, axis, split_axis=0, concat_axis=0, tiled=True)  58.7 us
    unnamed x8, waiting for transfers between devices  24.7 us
    ppermute x4, waiting for transfers between devices, gather_around(): earlier.append(lax.ppermute(earlier[-1], axis, up))  19.4 us
    unnamed x57, local copies, waits for them, and re-layouts  15 us
    ppermute x3, waiting for transfers between devices, gather_around(): later.append(lax.ppermute(later[-1], axis, down))  11.7 us
    ppermute x3, starting transfers between devices, gather_around(): later.append(lax.ppermute(later[-1], axis, down))  9.19 us
    add x4, other arithmetic, add_states(): return earlier + later  9.01 us
  transfers between devices with their start and end apart: 15, of which 12 were waited for; matrix products, arithmetic and copies ran while one was open for 13% of the time, Pallas kernels for 0%

profile of v1, /device:TPU:1, one launch (start us, length us, event | category | flops | bytes accessed | tf_op | source)
XLA Modules:
  0.0 301.1 jit_solution(17429279098058415954)
XLA Ops:
  10.4 19.0 %all-gather.15.cloned.1.call-done = f32[4,4,128,128]{3,2,1,0:T(8,128)} async-done(((f32[2,4,128,128]{3,2,1,0:T(8,128)}), f32[4,4,128,128]{3,2,1,0:T(8,128)}) %all-gather.15.cloned.1.call-update) | async-done | bytes 1048592 | tf_op jit(solution)/shard_map/all_gather | solution.py:34
  32.6 11.1 %collective-permute-done = bf16[2,192,512]{2,1,0:T(8,128)(2,1)S(1)} collective-permute-done((bf16[2,192,512]{2,1,0:T(8,128)(2,1)}, bf16[2,192,512]{2,1,0:T(8,128)(2,1)S(1)}, u32[]{:S(2)}, u32[]{:S(2)}) %collective-permute-start) | collective-permute-done | bytes 393248 | tf_op jit(solution)/shard_map/ppermute | solution.py:18
  43.7 2.7 collective-permute-start.4
  46.3 8.3 %collective-permute-done.1 = bf16[2,192,512]{2,1,0:T(8,128)(2,1)S(1)} collective-permute-done((bf16[2,192,512]{2,1,0:T(8,128)(2,1)S(1)}, bf16[2,192,512]{2,1,0:T(8,128)(2,1)S(1)}, u32[]{:S(2)}, u32[]{:S(2)}) %collective-permute-start.1) | collective-permute-done | bytes 393248 | tf_op jit(solution)/shard_map/ppermute | solution.py:18
  54.7 10.7 %all-gather.19.cloned.1.call-done = f32[8,4,128,128]{3,2,1,0:T(8,128)} async-done(((f32[2,4,128,128]{3,2,1,0:T(8,128)}), f32[8,4,128,128]{3,2,1,0:T(8,128)}) %all-gather.19.cloned.1.call-update) | async-done | bytes 2097168 | tf_op jit(solution)/shard_map/all_gather | solution.py:34
  65.4 2.5 fusion.35
  67.9 3.1 %collective-permute-start.5 = (bf16[2,192,512]{2,1,0:T(8,128)(2,1)S(1)}, bf16[2,192,512]{2,1,0:T(8,128)(2,1)S(1)}, u32[]{:S(2)}, u32[]{:S(2)}) collective-permute-start(bf16[2,192,512]{2,1,0:T(8,128)(2,1)S(1)} %collective-permute-done.4), channel_id=1, source_target_pairs={{0,7},{1,0},{2,1},{3,2},{4,3},{5,4},{6,5},{7,6},{8,15},{9,8},{10,9... | collective-permute-start | bytes 1179656 | tf_op jit(solution)/shard_map/ppermute | solution.py:20
  72.4 6.3 %collective-permute-done.5 = bf16[2,192,512]{2,1,0:T(8,128)(2,1)S(1)} collective-permute-done((bf16[2,192,512]{2,1,0:T(8,128)(2,1)S(1)}, bf16[2,192,512]{2,1,0:T(8,128)(2,1)S(1)}, u32[]{:S(2)}, u32[]{:S(2)}) %collective-permute-start.5) | collective-permute-done | bytes 393248 | tf_op jit(solution)/shard_map/ppermute | solution.py:20
  78.7 3.4 %collective-permute-start.6 = (bf16[2,192,512]{2,1,0:T(8,128)(2,1)S(1)}, bf16[2,192,512]{2,1,0:T(8,128)(2,1)S(1)}, u32[]{:S(2)}, u32[]{:S(2)}) collective-permute-start(bf16[2,192,512]{2,1,0:T(8,128)(2,1)S(1)} %collective-permute-done.5), channel_id=1, source_target_pairs={{0,7},{1,0},{2,1},{3,2},{4,3},{5,4},{6,5},{7,6},{8,15},{9,8},{10,9... | collective-permute-start | bytes 1179656 | tf_op jit(solution)/shard_map/ppermute | solution.py:20
  83.4 5.4 %collective-permute-done.6 = bf16[2,192,512]{2,1,0:T(8,128)(2,1)S(1)} collective-permute-done((bf16[2,192,512]{2,1,0:T(8,128)(2,1)S(1)}, bf16[2,192,512]{2,1,0:T(8,128)(2,1)S(1)}, u32[]{:S(2)}, u32[]{:S(2)}) %collective-permute-start.6) | collective-permute-done | bytes 393248 | tf_op jit(solution)/shard_map/ppermute | solution.py:20
  90.3 3.2 %copy-done.16 = bf16[2,192,8192]{2,1,0:T(8,128)(2,1)} copy-done((bf16[2,192,8192]{2,1,0:T(8,128)(2,1)}, bf16[2,192,8192]{2,1,0:T(8,128)(2,1)S(1)}, u32[]{:S(2)}) %copy-start.16) | copy-done | bytes 6291480
  93.5 2.7 fusion.5
  96.2 5.1 %all-gather.11.cloned.1.call-done = f32[4,2,4,128,128]{4,3,2,1,0:T(8,128)} async-done(((f32[1,2,4,128,128]{4,3,2,1,0:T(8,128)}), f32[4,2,4,128,128]{4,3,2,1,0:T(8,128)}) %all-gather.11.cloned.1.call-update) | async-done | bytes 2097168 | tf_op jit(solution)/shard_map/all_gather | solution.py:34
  108.9 15.4 %all-gather.17.cloned.1.call-done = f32[4,4,128,128]{3,2,1,0:T(8,128)} async-done(((f32[2,4,128,128]{3,2,1,0:T(8,128)}), f32[4,4,128,128]{3,2,1,0:T(8,128)}) %all-gather.17.cloned.1.call-update) | async-done | bytes 1048592 | tf_op jit(solution)/shard_map/all_gather | solution.py:34
  126.9 6.4 %bitcast_convert_fusion = bf16[512,4096]{1,0:T(8,128)(2,1)} fusion(bf16[2,192,8192]{2,1,0:T(8,128)(2,1)} %copy-done.16, s32[]{:T(128)S(6)} %select_n.199, bf16[2,4,24,8,128]{4,3,2,1,0:T(8,128)(2,1)S(1)} %fusion.41), kind=kOutput, calls=%fused_computation | convolution fusion | flops 1612709888 | bytes 7733252 | tf_op jit(solution)/shard_map/btr,btc->rc/dot_general | solution.py:107
  133.2 6.5 %copy.41 = bf16[512,4096]{0,1:T(8,128)(2,1)} copy(bf16[512,4096]{1,0:T(8,128)(2,1)} %bitcast_convert_fusion) | data formatting | bytes 8388608
  139.7 4.2 %convolution_convert_fusion = bf16[2,192,4096]{2,1,0:T(8,128)(2,1)S(1)} fusion(bf16[512,4096]{1,0:T(8,128)(2,1)} %param.8, bf16[2,4,24,8,128]{4,3,2,1,0:T(8,128)(2,1)S(1)} %fusion.41), kind=kOutput, calls=%fused_computation.1 | convolution fusion | flops 1612185600 | bytes 7733248 | tf_op jit(solution)/shard_map/btr,rc->btc/dot_general | solution.py:99
  145.9 6.5 %all-to-all-start = ((bf16[8,2,192,512]{3,2,1,0:T(8,128)(2,1)}), bf16[8,2,192,512]{3,2,1,0:T(8,128)(2,1)S(1)}, u32[]{:S(2)}, u32[]{:S(2)}) async-start(bf16[8,2,192,512]{3,2,1,0:T(8,128)(2,1)} %bitcast.228), calls=%async_computation | async-start | bytes 6291456 | tf_op jit(solution)/shard_map/all_to_all | solution.py:51
  152.4 7.8 %all-gather.21.cloned.1.call-done = f32[8,4,128,128]{3,2,1,0:T(8,128)} async-done(((f32[2,4,128,128]{3,2,1,0:T(8,128)}), f32[8,4,128,128]{3,2,1,0:T(8,128)}) %all-gather.21.cloned.1.call-update) | async-done | bytes 2097168 | tf_op jit(solution)/shard_map/all_gather | solution.py:34
  160.3 2.4 fusion.31
  168.0 58.7 %all-to-all-done = bf16[8,2,192,512]{3,2,1,0:T(8,128)(2,1)S(1)} async-done(((bf16[8,2,192,512]{3,2,1,0:T(8,128)(2,1)}), bf16[8,2,192,512]{3,2,1,0:T(8,128)(2,1)S(1)}, u32[]{:S(2)}, u32[]{:S(2)}) %all-to-all-start) | async-done | bytes 3145760 | tf_op jit(solution)/shard_map/all_to_all | solution.py:51
  228.0 24.6 %reduce-scatter.4.cloned.1.call-done = bf16[128,512]{1,0:T(8,128)(2,1)} async-done(((bf16[4096,512]{1,0:T(8,128)(2,1)}), bf16[128,512]{1,0:T(8,128)(2,1)}) %reduce-scatter.4.cloned.1.call-update) | async-done | bytes 131088
  254.3 34.3 %all-gather.13.cloned.1.call-done = f32[4,2,4,128,128]{4,3,2,1,0:T(8,128)} async-done(((f32[1,2,4,128,128]{4,3,2,1,0:T(8,128)}), f32[4,2,4,128,128]{4,3,2,1,0:T(8,128)}) %all-gather.13.cloned.1.call-update) | async-done | bytes 2097168 | tf_op jit(solution)/shard_map/all_gather | solution.py:34
  288.7 3.0 fusion.30
  (104 shorter events, 33.2 us)
Async XLA Ops:
  7.2 63.9 %copy-start.8 = (bf16[2,192,512]{2,1,0:T(8,128)(2,1)S(1)}, bf16[2,192,512]{2,1,0:T(8,128)(2,1)}, u32[]{:S(2)}) copy-start(bf16[2,192,512]{2,1,0:T(8,128)(2,1)} %param.6) | copy-start | bytes 1179652
  7.2 76.1 %copy-start.17 = (bf16[2,192,512]{2,1,0:T(8,128)(2,1)S(1)}, bf16[2,192,512]{2,1,0:T(8,128)(2,1)}, u32[]{:S(2)}) copy-start(bf16[2,192,512]{2,1,0:T(8,128)(2,1)} %param.9) | copy-start | bytes 1179652
  7.2 63.9 %copy-start.5 = (bf16[2,192,512]{2,1,0:T(8,128)(2,1)S(1)}, bf16[2,192,512]{2,1,0:T(8,128)(2,1)}, u32[]{:S(2)}) copy-start(bf16[2,192,512]{2,1,0:T(8,128)(2,1)} %param.5) | copy-start | bytes 1179652
  7.2 22.1 %all-gather.15.cloned.1.call-start = ((), (), s32[]{:S(2)}) async-start(), calls=%async_computation.4 | async-start | bytes 1572864 | tf_op jit(solution)/shard_map/all_gather | solution.py:34
  10.3 55.1 %all-gather.19.cloned.1.call-start = ((), (), s32[]{:S(2)}) async-start(), calls=%async_computation.6 | async-start | bytes 2621440 | tf_op jit(solution)/shard_map/all_gather | solution.py:34
  31.5 69.9 %all-gather.11.cloned.1.call-start = ((), (), s32[]{:S(2)}) async-start(), calls=%async_computation.2 | async-start | bytes 2621440 | tf_op jit(solution)/shard_map/all_gather | solution.py:34
  31.5 12.2 %collective-permute-start = (bf16[2,192,512]{2,1,0:T(8,128)(2,1)}, bf16[2,192,512]{2,1,0:T(8,128)(2,1)S(1)}, u32[]{:S(2)}, u32[]{:S(2)}) collective-permute-start(bf16[2,192,512]{2,1,0:T(8,128)(2,1)} %param.9), channel_id=1, source_target_pairs={{0,1},{1,2},{2,3},{3,4},{4,5},{5,6},{6,7},{7,0},{8,9},{9,10},{10,1... | collective-permute-start | bytes 1179656 | tf_op jit(solution)/shard_map/ppermute | solution.py:18
  43.7 11.0 %collective-permute-start.1 = (bf16[2,192,512]{2,1,0:T(8,128)(2,1)S(1)}, bf16[2,192,512]{2,1,0:T(8,128)(2,1)S(1)}, u32[]{:S(2)}, u32[]{:S(2)}) collective-permute-start(bf16[2,192,512]{2,1,0:T(8,128)(2,1)S(1)} %collective-permute-done), channel_id=1, source_target_pairs={{0,1},{1,2},{2,3},{3,4},{4,5},{5,6},{6,7},{7,0},{8,9},{9,10},{10,1... | collective-permute-start | bytes 1179656 | tf_op jit(solution)/shard_map/ppermute | solution.py:18
  43.7 24.3 %collective-permute-start.4 = (bf16[2,192,512]{2,1,0:T(8,128)(2,1)}, bf16[2,192,512]{2,1,0:T(8,128)(2,1)S(1)}, u32[]{:S(2)}, u32[]{:S(2)}) collective-permute-start(bf16[2,192,512]{2,1,0:T(8,128)(2,1)} %param.9), channel_id=1, source_target_pairs={{0,7},{1,0},{2,1},{3,2},{4,3},{5,4},{6,5},{7,6},{8,15},{9,8},{10,9... | collective-permute-start | bytes 1179656 | tf_op jit(solution)/shard_map/ppermute | solution.py:20
  54.7 16.4 %collective-permute-start.2 = (bf16[2,192,512]{2,1,0:T(8,128)(2,1)S(1)}, bf16[2,192,512]{2,1,0:T(8,128)(2,1)S(1)}, u32[]{:S(2)}, u32[]{:S(2)}) collective-permute-start(bf16[2,192,512]{2,1,0:T(8,128)(2,1)S(1)} %collective-permute-done.1), channel_id=1, source_target_pairs={{0,1},{1,2},{2,3},{3,4},{4,5},{5,6},{6,7},{7,0},{8,9},{9,10},{10,1... | collective-permute-start | bytes 1179656 | tf_op jit(solution)/shard_map/ppermute | solution.py:18
  67.9 56.4 %all-gather.17.cloned.1.call-start = ((), (), s32[]{:S(2)}) async-start(), calls=%async_computation.5 | async-start | bytes 1572864 | tf_op jit(solution)/shard_map/all_gather | solution.py:34
  67.9 10.7 %collective-permute-start.5 = (bf16[2,192,512]{2,1,0:T(8,128)(2,1)S(1)}, bf16[2,192,512]{2,1,0:T(8,128)(2,1)S(1)}, u32[]{:S(2)}, u32[]{:S(2)}) collective-permute-start(bf16[2,192,512]{2,1,0:T(8,128)(2,1)S(1)} %collective-permute-done.4), channel_id=1, source_target_pairs={{0,7},{1,0},{2,1},{3,2},{4,3},{5,4},{6,5},{7,6},{8,15},{9,8},{10,9... | collective-permute-start | bytes 1179656 | tf_op jit(solution)/shard_map/ppermute | solution.py:20
  71.0 11.0 %collective-permute-start.3 = (bf16[2,192,512]{2,1,0:T(8,128)(2,1)S(1)}, bf16[2,192,512]{2,1,0:T(8,128)(2,1)}, u32[]{:S(2)}, u32[]{:S(2)}) collective-permute-start(bf16[2,192,512]{2,1,0:T(8,128)(2,1)S(1)} %collective-permute-done.2), channel_id=1, source_target_pairs={{0,1},{1,2},{2,3},{3,4},{4,5},{5,6},{6,7},{7,0},{8,9},{9,10},{10,1... | collective-permute-start | bytes 1179656 | tf_op jit(solution)/shard_map/ppermute | solution.py:18
  72.4 21.1 %copy-start.19 = (bf16[512,4096]{1,0:T(8,128)(2,1)S(1)}, bf16[512,4096]{1,0:T(8,128)(2,1)}, u32[]{:S(2)}) copy-start(bf16[512,4096]{1,0:T(8,128)(2,1)} %param.8) | copy-start | bytes 12582916
  78.7 10.2 %collective-permute-start.6 = (bf16[2,192,512]{2,1,0:T(8,128)(2,1)S(1)}, bf16[2,192,512]{2,1,0:T(8,128)(2,1)S(1)}, u32[]{:S(2)}, u32[]{:S(2)}) collective-permute-start(bf16[2,192,512]{2,1,0:T(8,128)(2,1)S(1)} %collective-permute-done.5), channel_id=1, source_target_pairs={{0,7},{1,0},{2,1},{3,2},{4,3},{5,4},{6,5},{7,6},{8,15},{9,8},{10,9... | collective-permute-start | bytes 1179656 | tf_op jit(solution)/shard_map/ppermute | solution.py:20
  108.8 51.4 %all-gather.21.cloned.1.call-start = ((), (), s32[]{:S(2)}) async-start(), calls=%async_computation.7 | async-start | bytes 2621440 | tf_op jit(solution)/shard_map/all_gather | solution.py:34
  126.3 126.2 %reduce-scatter.4.cloned.1.call-start = ((), (), s32[]{:S(2)}) async-start(), calls=%async_computation.8 | async-start | bytes 4325376
  145.9 80.8 %all-to-all-start = ((bf16[8,2,192,512]{3,2,1,0:T(8,128)(2,1)}), bf16[8,2,192,512]{3,2,1,0:T(8,128)(2,1)S(1)}, u32[]{:S(2)}, u32[]{:S(2)}) async-start(bf16[8,2,192,512]{3,2,1,0:T(8,128)(2,1)} %bitcast.228), calls=%async_computation | async-start | bytes 6291456 | tf_op jit(solution)/shard_map/all_to_all | solution.py:51
  152.4 136.3 %all-gather.13.cloned.1.call-start = ((), (), s32[]{:S(2)}) async-start(), calls=%async_computation.3 | async-start | bytes 2621440 | tf_op jit(solution)/shard_map/all_gather | solution.py:34
  228.0 64.0 %copy-start.9 = (bf16[2,192,512]{2,1,0:T(8,128)(2,1)S(1)}, bf16[2,192,512]{2,1,0:T(8,128)(2,1)}, u32[]{:S(2)}) copy-start(bf16[2,192,512]{2,1,0:T(8,128)(2,1)} %param.6) | copy-start | bytes 1179652
  228.0 64.3 %copy-start.7 = (bf16[2,192,512]{2,1,0:T(8,128)(2,1)S(1)}, bf16[2,192,512]{2,1,0:T(8,128)(2,1)}, u32[]{:S(2)}) copy-start(bf16[2,192,512]{2,1,0:T(8,128)(2,1)} %param.5) | copy-start | bytes 1179652
  228.0 64.3 %copy-start.13 = (bf16[2,4,192,192]{3,2,1,0:T(8,128)(2,1)S(1)}, bf16[2,4,192,192]{3,2,1,0:T(8,128)(2,1)}, u32[]{:S(2)}) copy-start(bf16[2,4,192,192]{3,2,1,0:T(8,128)(2,1)} %copy-done.12) | copy-start | bytes 1769476
  228.0 64.8 %copy-start.3 = (bf16[2,4,192,128]{3,2,1,0:T(8,128)(2,1)S(1)}, bf16[2,4,192,128]{3,2,1,0:T(8,128)(2,1)}, u32[]{:S(2)}) copy-start(bf16[2,4,192,128]{3,2,1,0:T(8,128)(2,1)} %copy-done.2) | copy-start | bytes 1179652
  228.0 64.8 %copy-start.11 = (bf16[2,4,192,192]{3,2,1,0:T(8,128)(2,1)S(1)}, bf16[2,4,192,192]{3,2,1,0:T(8,128)(2,1)}, u32[]{:S(2)}) copy-start(bf16[2,4,192,192]{3,2,1,0:T(8,128)(2,1)} %select_convert_fusion.1) | copy-start | bytes 1769476
  (11 other events, 66.1 us)
Sparse Core Ops, SparseCore 0:
  10.4 18.8 all-gather.14
  31.6 33.7 all-gather.18
  68.0 33.3 all-gather.10
  108.9 15.3 all-gather.16
  126.5 33.7 all-gather.20
  164.0 88.4 reduce-scatter.3
  254.4 34.2 all-gather.12
